TPU v7x, 32 devices: a whole 2x2x4 slice. The times are simulated.
32 devices in a mesh: mem: 8 (over y, x, core), tile: 4 (over z).
Axes of the slice: x: 2, y: 2, z: 4, core: 2. Of those that a mesh axis runs over, the one named last changes fastest.
Arguments:
- perturb: bfloat16 [16, 6, 16, 64, 128], P('mem', None, None, 'tile'), may hold values from -2.5 to 2.5
- alpha: float32 [16, 16, 64, 128], P('mem', None, 'tile'), may hold values from -5 to 5
- alpha_mom: float32 [16, 16, 64, 128], P('mem', None, 'tile'), may hold values from -6 to 6
- static_ctl: float32 [6, 16, 64, 128], P(None, None, 'tile'), may hold values from -6 to 6
- static_mom: float32 [6, 16, 64, 128], P(None, 'mem', 'tile'), may hold values from -6 to 6
- loc_coef: float32 [2, 64, 128], P(None, 'tile'), may hold values from 0.04 to 0.36, as said below
- static_coef: float32 [2, 64, 128], P(None, 'tile'), may hold values from 0.04 to 0.36, as said below
- obs_cell: int32 [4, 1024], P('tile'), may hold values from 0 to 2047
- obs_mask: int32 [4, 1024], P('tile'), may hold values 0 or 1
- obs_value: float32 [6, 16, 4, 1024], P(None, None, 'tile'), may hold values from -6 to 6
- obs_weight: float32 [6, 16, 4, 1024], P(None, None, 'tile'), may hold values from 0.3 to 3
Outputs:
- new_alpha: float32 [16, 16, 64, 128], P('mem', None, 'tile')
- new_alpha_mom: float32 [16, 16, 64, 128], P('mem', None, 'tile')
- new_static: float32 [6, 16, 64, 128], P(None, 'mem', 'tile')
- new_static_mom: float32 [6, 16, 64, 128], P(None, 'mem', 'tile')
Inputs may be any that keep to these rules, and one draw needn't show every extreme that they name: `obs_cell`: slots of a tile may name the same cell. `loc_coef`: index 0 lies in 0.18 to 0.36, index 1 in 0.04 to 0.08. `static_coef`: index 0 lies in 0.18 to 0.36, index 1 in 0.04 to 0.08.
All inputs are finite; a program needn't handle non-finite values. No bound on the sum of `obs_mask` on one device may be relied on, other than what follows from the above.
Results may differ from a plain program's by a relative error of at most 0.0003.
Values sent between devices are 32-bit elements; how exact they have to be, the bound alone decides.
A program may use at most 64 MiB of HBM per device.

v0:
```python
import functools

import jax
import jax.numpy as jnp
from jax import lax
from jax.experimental import pallas as pl
from jax.experimental.pallas import tpu as pltpu
from jax.sharding import PartitionSpec as P

DIFF_STEPS = 12
LANES = 128
SUB = 8

momentum_rate = 0.9
step_rate = 0.5


def diffuse(src, bufs, coefs, height, block):
    center, down, right, left = coefs
    current = src
    for turn in range(DIFF_STEPS):
        target = bufs[turn % 2]
        low = turn + 1
        count = height + 2 * (DIFF_STEPS - 1 - turn)

        def rows(b, carry, current=current, target=target, low=low):
            i = low + b * block
            f = current[pl.ds(i, block)]
            above = current[pl.ds(i - 1, block)]
            below = current[pl.ds(i + 1, block)]
            new = center[pl.ds(i, block)] * f
            new = new + (down[pl.ds(i, block)] * below + down[pl.ds(i - 1, block)] * above)
            new = new + (
                right[pl.ds(i, block)] * pltpu.roll(f, LANES - 1, 3)
                + left[pl.ds(i, block)] * pltpu.roll(f, 1, 3)
            )
            target[pl.ds(i, block)] = new
            return carry

        lax.fori_loop(0, -(-count // block), rows, 0, unroll=True)
        current = target
    return current


def kernel(
    dims,
    perturb,
    alpha,
    loc_coef,
    static_coef,
    obs_cell,
    obs_mask,
    static_hbm,
    value_hbm,
    weight_hbm,
    out_alpha,
    out_static,
    field_a,
    field_b,
    ping_a0,
    ping_a1,
    field_s,
    field_g,
    ping_s0,
    ping_s1,
    coef_flat,
    coef_rows,
    coef_loc,
    coef_static,
    own_ctl,
    own_value,
    own_weight,
    matrix,
    obs_scale,
    obs_shift,
    static_flat,
    local_flat,
    part_own,
    part_pair,
    pair_in,
    chip_in,
    grads,
    load_sem,
    halo_send,
    halo_recv,
    pair_send,
    pair_recv,
    chip_send,
    chip_recv,
    gather_send,
    gather_recv,
    relay_send,
    relay_recv,
):
    mem_count, tile_count, members, variables, levels, height, stations = dims
    chips = mem_count // 2
    share = levels // mem_count
    fields = variables * share
    span = share * height
    static_vregs = field_s.shape[1]
    alpha_vregs = field_a.shape[1]
    mem = lax.axis_index("mem")
    tile = lax.axis_index("tile")
    chip = mem // 2
    core = lax.rem(mem, 2)
    partner = chip * 2 + (1 - core)
    first = mem * share
    halo = DIFF_STEPS
    has_low = tile > 0
    has_high = tile < tile_count - 1

    loads = [
        pltpu.make_async_copy(static_hbm.at[:, pl.ds(first, share)], own_ctl, load_sem.at[0]),
        pltpu.make_async_copy(value_hbm.at[:, pl.ds(first, share)], own_value, load_sem.at[1]),
        pltpu.make_async_copy(weight_hbm.at[:, pl.ds(first, share)], own_weight, load_sem.at[2]),
    ]
    for load in loads:
        load.start()

    barrier = pltpu.get_barrier_semaphore()
    pl.semaphore_signal(barrier, inc=1, device_id={"mem": partner})
    for k in range(1, chips):
        pl.semaphore_signal(
            barrier, inc=1, device_id={"mem": lax.rem(chip + k, chips) * 2 + core}
        )

    @pl.when(has_low)
    def _():
        pl.semaphore_signal(barrier, inc=1, device_id={"tile": tile - 1})

    @pl.when(has_high)
    def _():
        pl.semaphore_signal(barrier, inc=1, device_id={"tile": tile + 1})

    def up_copy(buf, slot):
        return pltpu.make_async_remote_copy(
            src_ref=buf.at[pl.ds(height, halo)],
            dst_ref=buf.at[pl.ds(0, halo)],
            send_sem=halo_send.at[slot, 0],
            recv_sem=halo_recv.at[slot, 0],
            device_id={"tile": tile + 1},
        )

    def down_copy(buf, slot):
        return pltpu.make_async_remote_copy(
            src_ref=buf.at[pl.ds(halo, halo)],
            dst_ref=buf.at[pl.ds(halo + height, halo)],
            send_sem=halo_send.at[slot, 1],
            recv_sem=halo_recv.at[slot, 1],
            device_id={"tile": tile - 1},
        )

    def halo_start(buf, slot):
        @pl.when(has_high)
        def _():
            up_copy(buf, slot).start()

        @pl.when(has_low)
        def _():
            down_copy(buf, slot).start()

    def halo_wait(buf, slot):
        @pl.when(has_high)
        def _():
            up_copy(buf, slot).wait_send()
            down_copy(buf, slot).wait_recv()

        @pl.when(has_low)
        def _():
            down_copy(buf, slot).wait_send()
            up_copy(buf, slot).wait_recv()

    def zero_edges(buf):
        @pl.when(tile == 0)
        def _():
            buf[pl.ds(0, halo)] = jnp.zeros((halo,) + buf.shape[1:], jnp.float32)

        @pl.when(tile == tile_count - 1)
        def _():
            buf[pl.ds(halo + height, halo)] = jnp.zeros((halo,) + buf.shape[1:], jnp.float32)

    def to_rows(flat, buf, vregs):
        for r in range(height):
            for b in range(vregs):
                buf[halo + r, b] = flat[pl.ds(b * SUB * height + r, SUB, stride=height), :]

    def from_rows(buf, flat, vregs):
        for r in range(height):
            for b in range(vregs):
                flat[pl.ds(b * SUB * height + r, SUB, stride=height), :] = buf[halo + r, b]

    coef_flat[...] = jnp.zeros(coef_flat.shape, jnp.float32)
    coef_flat[0 : 2 * height, :] = loc_coef[...]
    coef_flat[2 * height : 4 * height, :] = static_coef[...]
    for r in range(height):
        coef_rows[halo + r] = coef_flat[pl.ds(r, SUB, stride=height), :]
    to_rows(alpha, field_a, alpha_vregs)
    for buf in (field_a, field_b, field_s, field_g):
        zero_edges(buf)
    zero_edges(coef_rows)

    pl.semaphore_wait(barrier, chips + has_low.astype(jnp.int32) + has_high.astype(jnp.int32))

    halo_start(coef_rows, 0)
    halo_start(field_a, 1)

    for load in loads:
        load.wait()
    static_flat[...] = jnp.zeros(static_flat.shape, jnp.float32)
    static_flat[0 : fields * height, :] = own_ctl[...].reshape(fields * height, LANES)
    to_rows(static_flat, field_s, static_vregs)
    halo_start(field_s, 2)

    padded = static_vregs * SUB
    matrix[...] = jnp.zeros(matrix.shape, jnp.float32)
    mask = obs_mask[...].astype(jnp.float32)
    for v in range(variables):
        for l in range(share):
            f = v * share + l
            scaled = mask * own_weight[v, l]
            matrix[f : f + 1, :] = scaled
            matrix[padded + f : padded + f + 1, :] = scaled * own_value[v, l]
    whole = matrix[...]
    coarse = whole.astype(jnp.bfloat16).astype(jnp.float32)
    both = jnp.concatenate([coarse, whole - coarse], axis=0).astype(jnp.bfloat16)

    def cells(r, carry):
        number = lax.broadcasted_iota(jnp.int32, (LANES, stations), 0) + r * LANES
        hot = jnp.where(number == obs_cell[...], 1.0, 0.0).astype(jnp.bfloat16)
        sums = lax.dot_general(
            both, hot, (((1,), (1,)), ((), ())), preferred_element_type=jnp.float32
        )
        total = sums[: 2 * padded] + sums[2 * padded :]
        obs_scale[r] = total[:padded].reshape(static_vregs, SUB, LANES)
        obs_shift[r] = total[padded:].reshape(static_vregs, SUB, LANES)
        return carry

    lax.fori_loop(0, height, cells, 0)

    halo_wait(coef_rows, 0)
    extent = height * tile_count
    lane = lax.broadcasted_iota(jnp.int32, (SUB, SUB, LANES), 2)
    for which, coefs in ((0, coef_loc), (1, coef_static)):
        center, down, right, left = coefs.at[0], coefs.at[1], coefs.at[2], coefs.at[3]
        total_rows = 2 * halo + height
        shape = (SUB, SUB, LANES)
        for start in range(0, total_rows, SUB):
            position = lax.broadcasted_iota(jnp.int32, shape, 0) + (tile * height - halo + start)
            inside = (position >= 0) & (position < extent)
            x = jnp.broadcast_to(coef_rows[start : start + SUB, 2 * which : 2 * which + 1, :], shape)
            y = jnp.broadcast_to(
                coef_rows[start : start + SUB, 2 * which + 1 : 2 * which + 2, :], shape
            )
            if start == 0:
                before = jnp.concatenate([x[:1], x[:-1]], axis=0)
            else:
                before = jnp.broadcast_to(
                    coef_rows[start - 1 : start - 1 + SUB, 2 * which : 2 * which + 1, :], shape
                )
            before = jnp.where(position >= 1, before, 0.0)
            y_left = jnp.where(lane > 0, pltpu.roll(y, 1, 2), 0.0)
            down[start : start + SUB, 0] = jnp.where(
                (position >= 0) & (position < extent - 1), x, 0.0
            )
            center[start : start + SUB, 0] = jnp.where(
                inside, 1.0 - (x + before) - (y + y_left), 0.0
            )
            right[start : start + SUB, 0] = jnp.where(inside & (lane < LANES - 1), y, 0.0)
            left[start : start + SUB, 0] = jnp.where(inside, y_left, 0.0)
    loc_set = [coef_loc.at[n] for n in range(4)]
    static_set = [coef_static.at[n] for n in range(4)]

    halo_wait(field_a, 1)
    result = diffuse(field_a, (ping_a0, ping_a1), loc_set, height, 2)
    from_rows(result, local_flat, alpha_vregs)

    def ensemble(owner):
        offset = pl.multiple_of(owner * span, span)
        total = None
        for m in range(members):
            base = pl.multiple_of(m * levels * height + owner * span, span)
            field = local_flat[pl.ds(base, span), :]
            term = field[None] * perturb[m, :, pl.ds(offset, span), :].astype(jnp.float32)
            total = term if total is None else total + term
        return total

    def pair_copy(k):
        return pltpu.make_async_remote_copy(
            src_ref=part_pair.at[k],
            dst_ref=pair_in.at[k],
            send_sem=pair_send.at[k],
            recv_sem=pair_recv.at[k],
            device_id={"mem": partner},
        )

    def chip_copy(k):
        return pltpu.make_async_remote_copy(
            src_ref=part_own.at[k],
            dst_ref=chip_in.at[k],
            send_sem=chip_send.at[k],
            recv_sem=chip_recv.at[k],
            device_id={"mem": lax.rem(chip + k, chips) * 2 + core},
        )

    order = list(range(1, chips)) + [0]
    for k in order:
        owner_chip = lax.rem(chip + k, chips)
        part_pair[k] = ensemble(owner_chip * 2 + (1 - core))
        pair_copy(k).start()
    for k in order:
        owner_chip = lax.rem(chip + k, chips)
        mine = ensemble(owner_chip * 2 + core)
        pair_copy(k).wait_recv()
        part_own[k] = mine + pair_in[k]
        if k > 0:
            chip_copy(k).start()

    halo_wait(field_s, 2)
    static_part = diffuse(field_s, (ping_s0, ping_s1), static_set, height, 4)
    for k in order:
        pair_copy(k).wait_send()
    total = part_own[0]
    for k in range(1, chips):
        chip_copy(k).wait_recv()
        total = total + chip_in[k]
    static_flat[0 : fields * height, :] = total.reshape(fields * height, LANES)
    for r in range(height):
        for b in range(static_vregs):
            at = pl.ds(b * SUB * height + r, SUB, stride=height)
            increment = static_flat[at, :] + static_part[halo + r, b]
            field_g[halo + r, b] = obs_scale[r, b] * increment - obs_shift[r, b]
    halo_start(field_g, 3)
    from_rows(field_g, static_flat, static_vregs)
    grads[0, 0] = static_flat[0 : fields * height, :].reshape(variables, span, LANES)

    def gather_copy(k):
        return pltpu.make_async_remote_copy(
            src_ref=grads.at[0, 0],
            dst_ref=grads.at[0, k],
            send_sem=gather_send.at[k],
            recv_sem=gather_recv.at[k],
            device_id={"mem": lax.rem(chip + k, chips) * 2 + core},
        )

    def relay_copy(k):
        return pltpu.make_async_remote_copy(
            src_ref=grads.at[0, k],
            dst_ref=grads.at[1, k],
            send_sem=relay_send.at[k],
            recv_sem=relay_recv.at[k],
            device_id={"mem": partner},
        )

    for k in range(1, chips):
        gather_copy(k).start()
    relay_copy(0).start()

    def project(way, k):
        source = lax.rem(chip + chips - k, chips) * 2 + (core if way == 0 else 1 - core)
        offset = pl.multiple_of(source * span, span)
        for m in range(members):
            base = pl.multiple_of(m * levels * height + source * span, span)
            total = None
            for v in range(variables):
                weight = perturb[m, v, pl.ds(offset, span), :].astype(jnp.float32)
                term = weight * grads[way, k, v]
                total = term if total is None else total + term
            local_flat[pl.ds(base, span), :] = total

    project(0, 0)
    halo_wait(field_g, 3)
    result = diffuse(field_g, (ping_s0, ping_s1), static_set, height, 4)
    from_rows(result, static_flat, static_vregs)
    out_static[...] = static_flat[0 : fields * height, :]

    for k in range(1, chips):
        gather_copy(k).wait_recv()
        relay_copy(k).start()
        project(0, k)
    for k in range(chips):
        relay_copy(k).wait_recv()
        project(1, k)
    to_rows(local_flat, field_b, alpha_vregs)
    halo_start(field_b, 4)
    for k in range(1, chips):
        chip_copy(k).wait_send()
        gather_copy(k).wait_send()
    for k in range(chips):
        relay_copy(k).wait_send()
    halo_wait(field_b, 4)
    result = diffuse(field_b, (ping_a0, ping_a1), loc_set, height, 2)
    from_rows(result, out_alpha, alpha_vregs)


def local(
    perturb,
    alpha,
    alpha_mom,
    static_ctl,
    static_mom,
    loc_coef,
    static_coef,
    obs_cell,
    obs_mask,
    obs_value,
    obs_weight,
):
    mem_count = lax.axis_size("mem")
    tile_count = lax.axis_size("tile")
    members, variables, levels, height, width = perturb.shape
    stations = obs_cell.shape[1]
    chips = mem_count // 2
    share = levels // mem_count
    fields = variables * share
    span = share * height
    alpha_vregs = members * levels // SUB
    static_vregs = -(-fields // SUB)
    rows = 2 * DIFF_STEPS + height + 4
    dims = (mem_count, tile_count, members, variables, levels, height, stations)
    f32 = jnp.float32
    vmem = pl.BlockSpec(memory_space=pltpu.VMEM)
    anywhere = pl.BlockSpec(memory_space=pl.ANY)
    dma = pltpu.SemaphoreType.DMA
    chunk = (chips, variables, span, width)
    alpha_smooth, static_smooth = pl.pallas_call(
        functools.partial(kernel, dims),
        out_shape=(
            jax.ShapeDtypeStruct((members * levels * height, width), f32),
            jax.ShapeDtypeStruct((fields * height, width), f32),
        ),
        in_specs=[vmem] * 6 + [anywhere] * 3,
        out_specs=(vmem, vmem),
        scratch_shapes=[
            pltpu.VMEM((rows, alpha_vregs, SUB, width), f32),
            pltpu.VMEM((rows, alpha_vregs, SUB, width), f32),
            pltpu.VMEM((rows, alpha_vregs, SUB, width), f32),
            pltpu.VMEM((rows, alpha_vregs, SUB, width), f32),
            pltpu.VMEM((rows, static_vregs, SUB, width), f32),
            pltpu.VMEM((rows, static_vregs, SUB, width), f32),
            pltpu.VMEM((rows, static_vregs, SUB, width), f32),
            pltpu.VMEM((rows, static_vregs, SUB, width), f32),
            pltpu.VMEM((SUB * height, width), f32),
            pltpu.VMEM((rows, SUB, width), f32),
            pltpu.VMEM((4, rows, 1, SUB, width), f32),
            pltpu.VMEM((4, rows, 1, SUB, width), f32),
            pltpu.VMEM((variables, share, height, width), f32),
            pltpu.VMEM((variables, share, 1, stations), f32),
            pltpu.VMEM((variables, share, 1, stations), f32),
            pltpu.VMEM((2 * static_vregs * SUB, stations), f32),
            pltpu.VMEM((height, static_vregs, SUB, width), f32),
            pltpu.VMEM((height, static_vregs, SUB, width), f32),
            pltpu.VMEM((static_vregs * SUB * height, width), f32),
            pltpu.VMEM((members * levels * height, width), f32),
            pltpu.VMEM(chunk, f32),
            pltpu.VMEM(chunk, f32),
            pltpu.VMEM(chunk, f32),
            pltpu.VMEM(chunk, f32),
            pltpu.VMEM((2,) + chunk, f32),
            dma((3,)),
            dma((5, 2)),
            dma((5, 2)),
            dma((chips,)),
            dma((chips,)),
            dma((chips,)),
            dma((chips,)),
            dma((chips,)),
            dma((chips,)),
            dma((chips,)),
            dma((chips,)),
        ],
        compiler_params=pltpu.CompilerParams(
            collective_id=0, has_side_effects=True, vmem_limit_bytes=48 * 1024 * 1024
        ),
        name="analysis",
    )(
        perturb.reshape(members, variables, levels * height, width),
        alpha.reshape(members * levels * height, width),
        loc_coef.reshape(2 * height, width),
        static_coef.reshape(2 * height, width),
        obs_cell,
        obs_mask,
        static_ctl,
        obs_value,
        obs_weight,
    )
    own_ctl = lax.dynamic_slice_in_dim(static_ctl, lax.axis_index("mem") * share, share, 1)
    alpha_grad = alpha + alpha_smooth.reshape(alpha.shape)
    static_grad = own_ctl + static_smooth.reshape(own_ctl.shape)
    new_alpha_mom = momentum_rate * alpha_mom + alpha_grad
    new_alpha = alpha - step_rate * new_alpha_mom
    new_static_mom = momentum_rate * static_mom + static_grad
    new_static = own_ctl - step_rate * new_static_mom
    return (new_alpha, new_alpha_mom, new_static, new_static_mom)


def solution(mesh):
    return jax.shard_map(
        local,
        mesh=mesh,
        in_specs=(
            P("mem", None, None, "tile", None),
            P("mem", None, "tile", None),
            P("mem", None, "tile", None),
            P(None, None, "tile", None),
            P(None, "mem", "tile", None),
            P(None, "tile", None),
            P(None, "tile", None),
            P("tile", None),
            P("tile", None),
            P(None, None, "tile", None),
            P(None, None, "tile", None),
        ),
        out_specs=(
            P("mem", None, "tile", None),
            P("mem", None, "tile", None),
            P(None, "mem", "tile", None),
            P(None, "mem", "tile", None),
        ),
        check_vma=False,
    )
```

profile of v0, /device:TPU:0, one launch (start us, length us, event | category | flops | bytes accessed | tf_op | source)
XLA Modules:
  0.0 50.6 jit_solution(18256146246222038331)
XLA Ops:
  0.6 0.0 copy-start.7
  0.6 0.7 %copy-done.7 = s32[1,1024]{1,0:T(1,128)S(1)} copy-done((s32[1,1024]{1,0:T(1,128)S(1)}, s32[1,1024]{1,0:T(1,128)}, u32[]{:S(2)}) %copy-start.7) | copy-done | bytes 4120
  1.3 0.0 copy-start
  1.3 0.9 %copy-done = f32[2,16,16,128]{3,2,1,0:T(8,128)S(1)} copy-done((f32[2,16,16,128]{3,2,1,0:T(8,128)S(1)}, f32[2,16,16,128]{3,2,1,0:T(8,128)}, u32[]{:S(2)}) %copy-start) | copy-done | bytes 262168
  2.3 0.0 copy-start.1
  2.3 1.1 %copy-done.1 = f32[6,16,16,128]{3,2,1,0:T(8,128)S(1)} copy-done((f32[6,16,16,128]{3,2,1,0:T(8,128)S(1)}, f32[6,16,16,128]{3,2,1,0:T(8,128)}, u32[]{:S(2)}) %copy-start.1) | copy-done | bytes 786456
  3.4 0.0 copy-start.2
  3.4 1.1 %copy-done.2 = bf16[2,6,16,16,128]{4,3,2,1,0:T(8,128)(2,1)S(1)} copy-done((bf16[2,6,16,16,128]{4,3,2,1,0:T(8,128)(2,1)S(1)}, bf16[2,6,16,16,128]{4,3,2,1,0:T(8,128)(2,1)}, u32[]{:S(2)}) %copy-start.2) | copy-done | bytes 786456
  4.5 0.0 copy-start.3
  4.5 1.0 %copy-done.3 = f32[6,16,1,1024]{3,2,1,0:T(1,128)S(1)} copy-done((f32[6,16,1,1024]{3,2,1,0:T(1,128)S(1)}, f32[6,16,1,1024]{3,2,1,0:T(1,128)}, u32[]{:S(2)}) %copy-start.3) | copy-done | bytes 393240
  5.5 0.0 copy-start.4
  5.5 1.0 %copy-done.4 = f32[6,16,1,1024]{3,2,1,0:T(1,128)S(1)} copy-done((f32[6,16,1,1024]{3,2,1,0:T(1,128)S(1)}, f32[6,16,1,1024]{3,2,1,0:T(1,128)}, u32[]{:S(2)}) %copy-start.4) | copy-done | bytes 393240
  6.5 0.0 copy-start.5
  6.5 0.7 %copy-done.5 = f32[2,16,128]{2,1,0:T(8,128)S(1)} copy-done((f32[2,16,128]{2,1,0:T(8,128)S(1)}, f32[2,16,128]{2,1,0:T(8,128)}, u32[]{:S(2)}) %copy-start.5) | copy-done | bytes 16408
  7.3 0.0 copy-start.6
  7.3 0.7 %copy-done.6 = f32[2,16,128]{2,1,0:T(8,128)S(1)} copy-done((f32[2,16,128]{2,1,0:T(8,128)S(1)}, f32[2,16,128]{2,1,0:T(8,128)}, u32[]{:S(2)}) %copy-start.6) | copy-done | bytes 16408
  8.0 0.0 copy-start.8
  8.0 0.7 %copy-done.8 = s32[1,1024]{1,0:T(1,128)S(1)} copy-done((s32[1,1024]{1,0:T(1,128)S(1)}, s32[1,1024]{1,0:T(1,128)}, u32[]{:S(2)}) %copy-start.8) | copy-done | bytes 4120
  8.7 0.0 copy-start.9
  8.7 39.4 %analysis.1 = (f32[512,128]{1,0:T(8,128)S(1)}, f32[192,128]{1,0:T(8,128)S(1)}) custom-call(bf16[2,6,256,128]{3,2,1,0:T(8,128)(2,1)S(1)} %bitcast.7, f32[512,128]{1,0:T(8,128)S(1)} %bitcast.6, f32[32,128]{1,0:T(8,128)S(1)} %bitcast.10, f32[32,128]{1,0:T(8,128)S(1)} %bitcast.11, s32[1,1024]{1,0:T(1,128)S(1)} %copy-done.7, s32[1,1024]{1,0:T(1,128)S(1)} %copy-done.8, ...), custom_call_target="tpu_custom_call" | custom-call | tf_op jit(solution)/shard_map/analysis/pallas_call | solution.py:425
  48.1 0.0 copy-done.9
  48.1 0.0 copy-start.10
  48.1 0.9 %multiply_subtract_fusion = (f32[2,16,16,128]{3,2,1,0:T(8,128)}, f32[2,16,16,128]{3,2,1,0:T(8,128)}) fusion(f32[2,16,16,128]{3,2,1,0:T(8,128)S(1)} %copy-done, f32[2,16,16,128]{3,2,1,0:T(8,128)S(1)} %bitcast.8, f32[2,16,16,128]{3,2,1,0:T(8,128)S(1)} %copy-done.9), kind=kLoop, calls=%fused_computation | loop fusion | flops 327680 | bytes 1310720 | tf_op jit(solution)/shard_map/sub | solution.py:490
  49.0 0.0 copy-done.10
  49.0 1.6 %multiply_subtract_fusion.1 = (f32[6,2,16,128]{3,2,1,0:T(8,128)}, f32[6,2,16,128]{3,2,1,0:T(8,128)}) fusion(f32[6,16,16,128]{3,2,1,0:T(8,128)} %static_hbm.1, s32[]{:T(128)S(6)} %select_n.3, f32[6,2,16,128]{3,2,1,0:T(8,128)S(1)} %bitcast.9, f32[6,2,16,128]{3,2,1,0:T(8,128)S(1)} %copy-done.10), kind=kLoop, calls=%fused_computation.2 | loop fusion | flops 122880 | bytes 491524 | tf_op jit(solution)/shard_map/sub | solution.py:492
Async XLA Ops:
  0.6 0.7 %copy-start.7 = (s32[1,1024]{1,0:T(1,128)S(1)}, s32[1,1024]{1,0:T(1,128)}, u32[]{:S(2)}) copy-start(s32[1,1024]{1,0:T(1,128)} %obs_cell.1) | copy-start | bytes 12292
  1.3 0.9 %copy-start = (f32[2,16,16,128]{3,2,1,0:T(8,128)S(1)}, f32[2,16,16,128]{3,2,1,0:T(8,128)}, u32[]{:S(2)}) copy-start(f32[2,16,16,128]{3,2,1,0:T(8,128)} %param.12) | copy-start | bytes 786436
  2.3 1.1 %copy-start.1 = (f32[6,16,16,128]{3,2,1,0:T(8,128)S(1)}, f32[6,16,16,128]{3,2,1,0:T(8,128)}, u32[]{:S(2)}) copy-start(f32[6,16,16,128]{3,2,1,0:T(8,128)} %static_hbm.1) | copy-start | bytes 2359300
  3.4 1.1 %copy-start.2 = (bf16[2,6,16,16,128]{4,3,2,1,0:T(8,128)(2,1)S(1)}, bf16[2,6,16,16,128]{4,3,2,1,0:T(8,128)(2,1)}, u32[]{:S(2)}) copy-start(bf16[2,6,16,16,128]{4,3,2,1,0:T(8,128)(2,1)} %param.11) | copy-start | bytes 2359300
  4.5 1.0 %copy-start.3 = (f32[6,16,1,1024]{3,2,1,0:T(1,128)S(1)}, f32[6,16,1,1024]{3,2,1,0:T(1,128)}, u32[]{:S(2)}) copy-start(f32[6,16,1,1024]{3,2,1,0:T(1,128)} %value_hbm.1) | copy-start | bytes 1179652
  5.5 1.0 %copy-start.4 = (f32[6,16,1,1024]{3,2,1,0:T(1,128)S(1)}, f32[6,16,1,1024]{3,2,1,0:T(1,128)}, u32[]{:S(2)}) copy-start(f32[6,16,1,1024]{3,2,1,0:T(1,128)} %weight_hbm.1) | copy-start | bytes 1179652
  6.5 0.7 %copy-start.5 = (f32[2,16,128]{2,1,0:T(8,128)S(1)}, f32[2,16,128]{2,1,0:T(8,128)}, u32[]{:S(2)}) copy-start(f32[2,16,128]{2,1,0:T(8,128)} %param.16) | copy-start | bytes 49156
  7.3 0.7 %copy-start.6 = (f32[2,16,128]{2,1,0:T(8,128)S(1)}, f32[2,16,128]{2,1,0:T(8,128)}, u32[]{:S(2)}) copy-start(f32[2,16,128]{2,1,0:T(8,128)} %param.17) | copy-start | bytes 49156
  8.0 0.7 %copy-start.8 = (s32[1,1024]{1,0:T(1,128)S(1)}, s32[1,1024]{1,0:T(1,128)}, u32[]{:S(2)}) copy-start(s32[1,1024]{1,0:T(1,128)} %obs_mask.1) | copy-start | bytes 12292
  8.7 39.4 %copy-start.9 = (f32[2,16,16,128]{3,2,1,0:T(8,128)S(1)}, f32[2,16,16,128]{3,2,1,0:T(8,128)}, u32[]{:S(2)}) copy-start(f32[2,16,16,128]{3,2,1,0:T(8,128)} %param.13) | copy-start | bytes 786436
  48.1 0.9 %copy-start.10 = (f32[6,2,16,128]{3,2,1,0:T(8,128)S(1)}, f32[6,2,16,128]{3,2,1,0:T(8,128)}, u32[]{:S(2)}) copy-start(f32[6,2,16,128]{3,2,1,0:T(8,128)} %param.15) | copy-start | bytes 294916
where the time goes:
time: 51.1 us; the launch traced here: 50.6 us
  Pallas kernels  39.4 us (77%)
  local copies, waits for them, and re-layouts  8.04 us (16%)
  other arithmetic  2.45 us (5%)
  between operations  0.68 us (1%)
    pallas_call x1, Pallas kernels, local(): pl.pallas_call(functools.partial(kernel, dims), out_shape=(jax.ShapeDtype...  39.4 us
    unnamed x22, local copies, waits for them, and re-layouts  8.04 us
    sub x1, other arithmetic, local(): new_static = own_ctl - step_rate * new_static_mom  1.59 us

commit v1 on v0

--- a/solution.py
+++ b/solution.py
@@ -25,11 +25,11 @@
 
         def rows(b, carry, current=current, target=target, low=low):
             i = low + b * block
-            f = current[pl.ds(i, block)]
-            above = current[pl.ds(i - 1, block)]
-            below = current[pl.ds(i + 1, block)]
+            window = current[pl.ds(i - 1, block + 2)]
+            faces = down[pl.ds(i - 1, block + 1)]
+            f = window[1 : block + 1]
             new = center[pl.ds(i, block)] * f
-            new = new + (down[pl.ds(i, block)] * below + down[pl.ds(i - 1, block)] * above)
+            new = new + (faces[1:] * window[2:] + faces[:-1] * window[:-2])
             new = new + (
                 right[pl.ds(i, block)] * pltpu.roll(f, LANES - 1, 3)
                 + left[pl.ds(i, block)] * pltpu.roll(f, 1, 3)
@@ -44,17 +44,22 @@
 
 def kernel(
     dims,
-    perturb,
-    alpha,
-    loc_coef,
-    static_coef,
-    obs_cell,
-    obs_mask,
+    perturb_hbm,
+    alpha_hbm,
+    loc_hbm,
+    coef_hbm,
+    cell_hbm,
+    mask_hbm,
     static_hbm,
     value_hbm,
     weight_hbm,
     out_alpha,
     out_static,
+    alpha,
+    own_ctl,
+    perturb,
+    obs_cell,
+    obs_mask,
     field_a,
     field_b,
     ping_a0,
@@ -67,7 +72,6 @@
     coef_rows,
     coef_loc,
     coef_static,
-    own_ctl,
     own_value,
     own_weight,
     matrix,
@@ -109,10 +113,20 @@
     has_low = tile > 0
     has_high = tile < tile_count - 1
 
+    sources = [
+        (loc_hbm, coef_flat.at[pl.ds(0, 2 * height)]),
+        (coef_hbm, coef_flat.at[pl.ds(2 * height, 2 * height)]),
+        (alpha_hbm, alpha),
+        (static_hbm.at[:, pl.ds(first, share)], own_ctl),
+        (cell_hbm, obs_cell),
+        (mask_hbm, obs_mask),
+        (value_hbm.at[:, pl.ds(first, share)], own_value),
+        (weight_hbm.at[:, pl.ds(first, share)], own_weight),
+        (perturb_hbm, perturb),
+    ]
     loads = [
-        pltpu.make_async_copy(static_hbm.at[:, pl.ds(first, share)], own_ctl, load_sem.at[0]),
-        pltpu.make_async_copy(value_hbm.at[:, pl.ds(first, share)], own_value, load_sem.at[1]),
-        pltpu.make_async_copy(weight_hbm.at[:, pl.ds(first, share)], own_weight, load_sem.at[2]),
+        pltpu.make_async_copy(source, target, load_sem.at[n])
+        for n, (source, target) in enumerate(sources)
     ]
     for load in loads:
         load.start()
@@ -189,9 +203,9 @@
             for b in range(vregs):
                 flat[pl.ds(b * SUB * height + r, SUB, stride=height), :] = buf[halo + r, b]
 
-    coef_flat[...] = jnp.zeros(coef_flat.shape, jnp.float32)
-    coef_flat[0 : 2 * height, :] = loc_coef[...]
-    coef_flat[2 * height : 4 * height, :] = static_coef[...]
+    coef_flat[4 * height :, :] = jnp.zeros((4 * height, LANES), jnp.float32)
+    for load in loads[:3]:
+        load.wait()
     for r in range(height):
         coef_rows[halo + r] = coef_flat[pl.ds(r, SUB, stride=height), :]
     to_rows(alpha, field_a, alpha_vregs)
@@ -204,13 +218,14 @@
     halo_start(coef_rows, 0)
     halo_start(field_a, 1)
 
-    for load in loads:
-        load.wait()
+    loads[3].wait()
     static_flat[...] = jnp.zeros(static_flat.shape, jnp.float32)
     static_flat[0 : fields * height, :] = own_ctl[...].reshape(fields * height, LANES)
     to_rows(static_flat, field_s, static_vregs)
     halo_start(field_s, 2)
 
+    for load in loads[4:]:
+        load.wait()
     padded = static_vregs * SUB
     matrix[...] = jnp.zeros(matrix.shape, jnp.float32)
     mask = obs_mask[...].astype(jnp.float32)
@@ -419,18 +434,23 @@
     dims = (mem_count, tile_count, members, variables, levels, height, stations)
     f32 = jnp.float32
     vmem = pl.BlockSpec(memory_space=pltpu.VMEM)
-    anywhere = pl.BlockSpec(memory_space=pl.ANY)
+    in_hbm = pl.BlockSpec(memory_space=pltpu.HBM)
     dma = pltpu.SemaphoreType.DMA
     chunk = (chips, variables, span, width)
-    alpha_smooth, static_smooth = pl.pallas_call(
+    alpha_smooth, static_smooth, alpha_copy, own_ctl = pl.pallas_call(
         functools.partial(kernel, dims),
         out_shape=(
             jax.ShapeDtypeStruct((members * levels * height, width), f32),
             jax.ShapeDtypeStruct((fields * height, width), f32),
+            jax.ShapeDtypeStruct((members * levels * height, width), f32),
+            jax.ShapeDtypeStruct((variables, share, height, width), f32),
         ),
-        in_specs=[vmem] * 6 + [anywhere] * 3,
-        out_specs=(vmem, vmem),
+        in_specs=[in_hbm] * 9,
+        out_specs=(vmem,) * 4,
         scratch_shapes=[
+            pltpu.VMEM((members, variables, levels * height, width), perturb.dtype),
+            pltpu.VMEM(obs_cell.shape, obs_cell.dtype),
+            pltpu.VMEM(obs_mask.shape, obs_mask.dtype),
             pltpu.VMEM((rows, alpha_vregs, SUB, width), f32),
             pltpu.VMEM((rows, alpha_vregs, SUB, width), f32),
             pltpu.VMEM((rows, alpha_vregs, SUB, width), f32),
@@ -443,7 +463,6 @@
             pltpu.VMEM((rows, SUB, width), f32),
             pltpu.VMEM((4, rows, 1, SUB, width), f32),
             pltpu.VMEM((4, rows, 1, SUB, width), f32),
-            pltpu.VMEM((variables, share, height, width), f32),
             pltpu.VMEM((variables, share, 1, stations), f32),
             pltpu.VMEM((variables, share, 1, stations), f32),
             pltpu.VMEM((2 * static_vregs * SUB, stations), f32),
@@ -456,7 +475,7 @@
             pltpu.VMEM(chunk, f32),
             pltpu.VMEM(chunk, f32),
             pltpu.VMEM((2,) + chunk, f32),
-            dma((3,)),
+            dma((9,)),
             dma((5, 2)),
             dma((5, 2)),
             dma((chips,)),
@@ -469,7 +488,7 @@
             dma((chips,)),
         ],
         compiler_params=pltpu.CompilerParams(
-            collective_id=0, has_side_effects=True, vmem_limit_bytes=48 * 1024 * 1024
+            collective_id=0, has_side_effects=True, vmem_limit_bytes=60 * 1024 * 1024
         ),
         name="analysis",
     )(
@@ -483,7 +502,7 @@
         obs_value,
         obs_weight,
     )
-    own_ctl = lax.dynamic_slice_in_dim(static_ctl, lax.axis_index("mem") * share, share, 1)
+    alpha = alpha_copy.reshape(alpha.shape)
     alpha_grad = alpha + alpha_smooth.reshape(alpha.shape)
     static_grad = own_ctl + static_smooth.reshape(own_ctl.shape)
     new_alpha_mom = momentum_rate * alpha_mom + alpha_grad

time: 51.1 us -> 43.7 us (0.86)
  local copies, waits for them, and re-layouts: 8.04 us -> 0.02 us
  Pallas kernels: 39.4 us -> 40.2 us
    unnamed x22 -> x8, local copies, waits for them, and re-layouts: 8.04 us -> 0.02 us
    sub x1, other arithmetic: 0.86 us -> 1.93 us  [local(): new_alpha = alpha - step_rate * new_alpha_mom]
    sub x1, other arithmetic: 1.59 us -> 0.7 us  [local(): new_static = own_ctl - step_rate * new_static_mom]
    pallas_call x1, Pallas kernels: 39.4 us -> 40.2 us  [local(): pl.pallas_call(functools.partial(kernel, dims), out_shape=(jax.ShapeDtype...]
where the time goes in v1:
time: 43.7 us; the launch traced here: 43.5 us
  Pallas kernels  40.2 us (92%)
  other arithmetic  2.62 us (6%)
  between operations  0.69 us (2%)
    pallas_call x1, Pallas kernels, local(): pl.pallas_call(functools.partial(kernel, dims), out_shape=(jax.ShapeDtype...  40.2 us
    sub x1, other arithmetic, local(): new_alpha = alpha - step_rate * new_alpha_mom  1.93 us

profile of v1, /device:TPU:0, one launch (start us, length us, event | category | flops | bytes accessed | tf_op | source)
XLA Modules:
  0.0 43.5 jit_solution(12462215447924569918)
XLA Ops:
  0.6 0.0 copy-start
  0.6 40.2 %analysis.1 = (f32[512,128]{1,0:T(8,128)}, f32[192,128]{1,0:T(8,128)}, f32[512,128]{1,0:T(8,128)}, f32[6,2,16,128]{3,2,1,0:T(8,128)}) custom-call(bf16[2,6,256,128]{3,2,1,0:T(8,128)(2,1)} %bitcast.7, f32[512,128]{1,0:T(8,128)} %bitcast.10, f32[32,128]{1,0:T(8,128)} %bitcast.12, f32[32,128]{1,0:T(8,128)} %bitcast.13, s32[1,1024]{1,0:T(1,128)} %cell_hbm.1, ...), custom_call_target="tpu_custom_call" | custom-call | tf_op jit(solution)/shard_map/analysis/pallas_call | solution.py:440
  40.8 0.0 copy-done
  40.9 0.0 copy-start.1
  40.9 0.0 copy-start.2
  40.9 0.0 copy-start.3
  40.9 1.9 %multiply_subtract_fusion = (f32[2,16,16,128]{3,2,1,0:T(8,128)}, f32[2,16,16,128]{3,2,1,0:T(8,128)}) fusion(f32[2,16,16,128]{3,2,1,0:T(8,128)} %bitcast.9, f32[2,16,16,128]{3,2,1,0:T(8,128)} %bitcast.8, f32[2,16,16,128]{3,2,1,0:T(8,128)S(1)} %copy-done), kind=kLoop, calls=%fused_computation | loop fusion | flops 327680 | bytes 1310720 | tf_op jit(solution)/shard_map/sub | solution.py:509
  42.8 0.0 copy-done.1
  42.8 0.0 copy-done.2
  42.8 0.0 copy-done.3
  42.8 0.7 %multiply_subtract_fusion.1 = (f32[6,2,16,128]{3,2,1,0:T(8,128)}, f32[6,2,16,128]{3,2,1,0:T(8,128)}) fusion(f32[6,2,16,128]{3,2,1,0:T(8,128)S(1)} %copy-done.3, f32[6,2,16,128]{3,2,1,0:T(8,128)S(1)} %bitcast.11, f32[6,2,16,128]{3,2,1,0:T(8,128)S(1)} %copy-done.1), kind=kLoop, calls=%fused_computation.2 | loop fusion | flops 122880 | bytes 491520 | tf_op jit(solution)/shard_map/sub | solution.py:511
Async XLA Ops:
  0.6 40.2 %copy-start = (f32[2,16,16,128]{3,2,1,0:T(8,128)S(1)}, f32[2,16,16,128]{3,2,1,0:T(8,128)}, u32[]{:S(2)}) copy-start(f32[2,16,16,128]{3,2,1,0:T(8,128)} %param.13) | copy-start | bytes 786436
  40.9 2.0 %copy-start.1 = (f32[6,2,16,128]{3,2,1,0:T(8,128)S(1)}, f32[6,2,16,128]{3,2,1,0:T(8,128)}, u32[]{:S(2)}) copy-start(f32[6,2,16,128]{3,2,1,0:T(8,128)} %param.15) | copy-start | bytes 294916
  40.9 2.0 %copy-start.2 = (f32[192,128]{1,0:T(8,128)S(1)}, f32[192,128]{1,0:T(8,128)}, u32[]{:S(2)}) copy-start(f32[192,128]{1,0:T(8,128)} %get-tuple-element.11) | copy-start | bytes 294916
  40.9 1.9 %copy-start.3 = (f32[6,2,16,128]{3,2,1,0:T(8,128)S(1)}, f32[6,2,16,128]{3,2,1,0:T(8,128)}, u32[]{:S(2)}) copy-start(f32[6,2,16,128]{3,2,1,0:T(8,128)} %get-tuple-element.10) | copy-start | bytes 294916

commit v2 on v1

--- a/solution.py
+++ b/solution.py
@@ -55,8 +55,8 @@
     weight_hbm,
     out_alpha,
     out_static,
+    own_ctl,
     alpha,
-    own_ctl,
     perturb,
     obs_cell,
     obs_mask,
@@ -102,7 +102,7 @@
     fields = variables * share
     span = share * height
     static_vregs = field_s.shape[1]
-    alpha_vregs = field_a.shape[1]
+    alpha_vregs = field_a.shape[0]
     mem = lax.axis_index("mem")
     tile = lax.axis_index("tile")
     chip = mem // 2
@@ -208,15 +208,30 @@
         load.wait()
     for r in range(height):
         coef_rows[halo + r] = coef_flat[pl.ds(r, SUB, stride=height), :]
-    to_rows(alpha, field_a, alpha_vregs)
-    for buf in (field_a, field_b, field_s, field_g):
+    group_rows = SUB * height
+    groups_a = [field_a.at[g] for g in range(alpha_vregs)]
+    groups_b = [field_b.at[g] for g in range(alpha_vregs)]
+
+    def group_in(flat, g):
+        for r in range(height):
+            field = flat[pl.ds(g * group_rows + r, SUB, stride=height), :]
+            (field_a if flat is alpha else field_b)[g, halo + r, 0] = field
+
+    def group_out(result, flat, g):
+        for r in range(height):
+            flat[pl.ds(g * group_rows + r, SUB, stride=height), :] = result[halo + r, 0]
+
+    for g in range(alpha_vregs):
+        group_in(alpha, g)
+    for buf in groups_a + groups_b + [field_s, field_g]:
         zero_edges(buf)
     zero_edges(coef_rows)
 
     pl.semaphore_wait(barrier, chips + has_low.astype(jnp.int32) + has_high.astype(jnp.int32))
 
     halo_start(coef_rows, 0)
-    halo_start(field_a, 1)
+    for g in range(alpha_vregs):
+        halo_start(groups_a[g], 4 + g)
 
     loads[3].wait()
     static_flat[...] = jnp.zeros(static_flat.shape, jnp.float32)
@@ -250,7 +265,7 @@
         obs_shift[r] = total[padded:].reshape(static_vregs, SUB, LANES)
         return carry
 
-    lax.fori_loop(0, height, cells, 0)
+    lax.fori_loop(0, height // 2, cells, 0)
 
     halo_wait(coef_rows, 0)
     extent = height * tile_count
@@ -285,9 +300,10 @@
     loc_set = [coef_loc.at[n] for n in range(4)]
     static_set = [coef_static.at[n] for n in range(4)]
 
-    halo_wait(field_a, 1)
-    result = diffuse(field_a, (ping_a0, ping_a1), loc_set, height, 2)
-    from_rows(result, local_flat, alpha_vregs)
+    for g in range(alpha_vregs):
+        halo_wait(groups_a[g], 4 + g)
+        result = diffuse(groups_a[g], (ping_a0, ping_a1), loc_set, height, 4)
+        group_out(result, local_flat, g)
 
     def ensemble(owner):
         offset = pl.multiple_of(owner * span, span)
@@ -330,6 +346,7 @@
         if k > 0:
             chip_copy(k).start()
 
+    lax.fori_loop(height // 2, height, cells, 0)
     halo_wait(field_s, 2)
     static_part = diffuse(field_s, (ping_s0, ping_s1), static_set, height, 4)
     for k in order:
@@ -395,16 +412,18 @@
     for k in range(chips):
         relay_copy(k).wait_recv()
         project(1, k)
-    to_rows(local_flat, field_b, alpha_vregs)
-    halo_start(field_b, 4)
+    for g in range(alpha_vregs):
+        group_in(local_flat, g)
+        halo_start(groups_b[g], 4 + alpha_vregs + g)
     for k in range(1, chips):
         chip_copy(k).wait_send()
         gather_copy(k).wait_send()
     for k in range(chips):
         relay_copy(k).wait_send()
-    halo_wait(field_b, 4)
-    result = diffuse(field_b, (ping_a0, ping_a1), loc_set, height, 2)
-    from_rows(result, out_alpha, alpha_vregs)
+    for g in range(alpha_vregs):
+        halo_wait(groups_b[g], 4 + alpha_vregs + g)
+        result = diffuse(groups_b[g], (ping_a0, ping_a1), loc_set, height, 4)
+        group_out(result, out_alpha, g)
 
 
 def local(
@@ -437,24 +456,24 @@
     in_hbm = pl.BlockSpec(memory_space=pltpu.HBM)
     dma = pltpu.SemaphoreType.DMA
     chunk = (chips, variables, span, width)
-    alpha_smooth, static_smooth, alpha_copy, own_ctl = pl.pallas_call(
+    alpha_smooth, static_smooth, own_ctl = pl.pallas_call(
         functools.partial(kernel, dims),
         out_shape=(
             jax.ShapeDtypeStruct((members * levels * height, width), f32),
             jax.ShapeDtypeStruct((fields * height, width), f32),
-            jax.ShapeDtypeStruct((members * levels * height, width), f32),
             jax.ShapeDtypeStruct((variables, share, height, width), f32),
         ),
         in_specs=[in_hbm] * 9,
-        out_specs=(vmem,) * 4,
+        out_specs=(vmem,) * 3,
         scratch_shapes=[
+            pltpu.VMEM((members * levels * height, width), f32),
             pltpu.VMEM((members, variables, levels * height, width), perturb.dtype),
             pltpu.VMEM(obs_cell.shape, obs_cell.dtype),
             pltpu.VMEM(obs_mask.shape, obs_mask.dtype),
-            pltpu.VMEM((rows, alpha_vregs, SUB, width), f32),
-            pltpu.VMEM((rows, alpha_vregs, SUB, width), f32),
-            pltpu.VMEM((rows, alpha_vregs, SUB, width), f32),
-            pltpu.VMEM((rows, alpha_vregs, SUB, width), f32),
+            pltpu.VMEM((alpha_vregs, rows, 1, SUB, width), f32),
+            pltpu.VMEM((alpha_vregs, rows, 1, SUB, width), f32),
+            pltpu.VMEM((rows, 1, SUB, width), f32),
+            pltpu.VMEM((rows, 1, SUB, width), f32),
             pltpu.VMEM((rows, static_vregs, SUB, width), f32),
             pltpu.VMEM((rows, static_vregs, SUB, width), f32),
             pltpu.VMEM((rows, static_vregs, SUB, width), f32),
@@ -476,8 +495,8 @@
             pltpu.VMEM(chunk, f32),
             pltpu.VMEM((2,) + chunk, f32),
             dma((9,)),
-            dma((5, 2)),
-            dma((5, 2)),
+            dma((4 + 2 * alpha_vregs, 2)),
+            dma((4 + 2 * alpha_vregs, 2)),
             dma((chips,)),
             dma((chips,)),
             dma((chips,)),
@@ -502,7 +521,6 @@
         obs_value,
         obs_weight,
     )
-    alpha = alpha_copy.reshape(alpha.shape)
     alpha_grad = alpha + alpha_smooth.reshape(alpha.shape)
     static_grad = own_ctl + static_smooth.reshape(own_ctl.shape)
     new_alpha_mom = momentum_rate * alpha_mom + alpha_grad

time: 43.7 us -> 41.4 us (0.947)
  Pallas kernels: 40.2 us -> 37 us
  other arithmetic: 2.62 us -> 3.47 us
    pallas_call x1, Pallas kernels: 40.2 us -> 37 us  [local(): pl.pallas_call(functools.partial(kernel, dims), out_shape=(jax.ShapeDtype...]
    sub x1, other arithmetic: 0.7 us -> 1.68 us  [local(): new_static = own_ctl - step_rate * new_static_mom]
where the time goes in v2:
time: 41.4 us; the launch traced here: 41.2 us
  Pallas kernels  37 us (89%)
  other arithmetic  3.47 us (8%)
  between operations  0.68 us (2%)
    pallas_call x1, Pallas kernels, local(): pl.pallas_call(functools.partial(kernel, dims), out_shape=(jax.ShapeDtype...  37 us
    sub x1, other arithmetic, local(): new_alpha = alpha - step_rate * new_alpha_mom  1.79 us
    sub x1, other arithmetic, local(): new_static = own_ctl - step_rate * new_static_mom  1.68 us

profile of v2, /device:TPU:0, one launch (start us, length us, event | category | flops | bytes accessed | tf_op | source)
XLA Modules:
  0.0 41.2 jit_solution(5777797732480543509)
XLA Ops:
  0.6 0.0 copy-start.2
  0.6 0.0 copy-start.1
  0.7 37.0 %analysis.1 = (f32[512,128]{1,0:T(8,128)}, f32[192,128]{1,0:T(8,128)}, f32[6,2,16,128]{3,2,1,0:T(8,128)}) custom-call(bf16[2,6,256,128]{3,2,1,0:T(8,128)(2,1)} %bitcast.7, f32[512,128]{1,0:T(8,128)} %bitcast.6, f32[32,128]{1,0:T(8,128)} %bitcast.10, f32[32,128]{1,0:T(8,128)} %bitcast.11, s32[1,1024]{1,0:T(1,128)} %cell_hbm.1, s32[1,1024]{1,0:T(1,128)} %mask_hbm.1, ...), custom_call_target="tpu_custom_call" | custom-call | tf_op jit(solution)/shard_map/analysis/pallas_call | solution.py:459
  37.7 0.0 copy-start
  37.7 0.0 copy-done.2
  37.7 1.7 %multiply_subtract_fusion.1 = (f32[6,2,16,128]{3,2,1,0:T(8,128)}, f32[6,2,16,128]{3,2,1,0:T(8,128)}) fusion(f32[6,2,16,128]{3,2,1,0:T(8,128)} %get-tuple-element.8, f32[6,2,16,128]{3,2,1,0:T(8,128)} %bitcast.9, f32[6,2,16,128]{3,2,1,0:T(8,128)S(1)} %copy-done.2), kind=kLoop, calls=%fused_computation.2 | loop fusion | flops 122880 | bytes 491520 | tf_op jit(solution)/shard_map/sub | solution.py:529
  39.4 0.0 copy-done.1
  39.4 0.0 copy-done
  39.4 1.8 %multiply_subtract_fusion = (f32[2,16,16,128]{3,2,1,0:T(8,128)}, f32[2,16,16,128]{3,2,1,0:T(8,128)}) fusion(f32[2,16,16,128]{3,2,1,0:T(8,128)S(1)} %copy-done, f32[2,16,16,128]{3,2,1,0:T(8,128)} %bitcast.8, f32[2,16,16,128]{3,2,1,0:T(8,128)S(1)} %copy-done.1), kind=kLoop, calls=%fused_computation | loop fusion | flops 327680 | bytes 1310720 | tf_op jit(solution)/shard_map/sub | solution.py:527
Async XLA Ops:
  0.6 37.1 %copy-start.2 = (f32[6,2,16,128]{3,2,1,0:T(8,128)S(1)}, f32[6,2,16,128]{3,2,1,0:T(8,128)}, u32[]{:S(2)}) copy-start(f32[6,2,16,128]{3,2,1,0:T(8,128)} %param.15) | copy-start | bytes 294916
  0.6 38.7 %copy-start.1 = (f32[2,16,16,128]{3,2,1,0:T(8,128)S(1)}, f32[2,16,16,128]{3,2,1,0:T(8,128)}, u32[]{:S(2)}) copy-start(f32[2,16,16,128]{3,2,1,0:T(8,128)} %param.13) | copy-start | bytes 786436
  37.7 1.7 %copy-start = (f32[2,16,16,128]{3,2,1,0:T(8,128)S(1)}, f32[2,16,16,128]{3,2,1,0:T(8,128)}, u32[]{:S(2)}) copy-start(f32[2,16,16,128]{3,2,1,0:T(8,128)} %param.12) | copy-start | bytes 786436

commit v3 on v2

--- a/solution.py
+++ b/solution.py
@@ -424,6 +424,16 @@
         halo_wait(groups_b[g], 4 + alpha_vregs + g)
         result = diffuse(groups_b[g], (ping_a0, ping_a1), loc_set, height, 4)
         group_out(result, out_alpha, g)
+
+
+def update(field_a, mom_a, smooth_a, field_s, mom_s, smooth_s, new_a, new_mom_a, new_s, new_mom_s):
+    for field, mom, smooth, new, new_mom in (
+        (field_a, mom_a, smooth_a, new_a, new_mom_a),
+        (field_s, mom_s, smooth_s, new_s, new_mom_s),
+    ):
+        moved = momentum_rate * mom[...] + (field[...] + smooth[...])
+        new_mom[...] = moved
+        new[...] = field[...] - step_rate * moved
 
 
 def local(
@@ -521,12 +531,22 @@
         obs_value,
         obs_weight,
     )
-    alpha_grad = alpha + alpha_smooth.reshape(alpha.shape)
-    static_grad = own_ctl + static_smooth.reshape(own_ctl.shape)
-    new_alpha_mom = momentum_rate * alpha_mom + alpha_grad
-    new_alpha = alpha - step_rate * new_alpha_mom
-    new_static_mom = momentum_rate * static_mom + static_grad
-    new_static = own_ctl - step_rate * new_static_mom
+    like = jax.ShapeDtypeStruct
+    new_alpha, new_alpha_mom, new_static, new_static_mom = pl.pallas_call(
+        update,
+        out_shape=(like(alpha.shape, f32),) * 2 + (like(own_ctl.shape, f32),) * 2,
+        in_specs=[vmem] * 6,
+        out_specs=(vmem,) * 4,
+        compiler_params=pltpu.CompilerParams(vmem_limit_bytes=60 * 1024 * 1024),
+        name="update",
+    )(
+        alpha,
+        alpha_mom,
+        alpha_smooth.reshape(alpha.shape),
+        own_ctl,
+        static_mom,
+        static_smooth.reshape(own_ctl.shape),
+    )
     return (new_alpha, new_alpha_mom, new_static, new_static_mom)
 
 

time: 41.4 us -> 40 us (0.966)
  other arithmetic: 3.47 us -> 0 us
  Pallas kernels: 37 us -> 39.1 us
    sub x2 -> x0, other arithmetic: 3.47 us -> none  [the longest x1 1.79 us: local(): new_alpha = alpha - step_rate * new_alpha_mom]
    pallas_call x0 -> x1, Pallas kernels: none -> 2.1 us  [local(): pl.pallas_call(update, out_shape=(like(alpha.shape, f32),) * 2 + (like(ow...]
where the time goes in v3:
time: 40 us; the launch traced here: 39.8 us
  Pallas kernels  39.1 us (98%)
  between operations  0.64 us (2%)
    pallas_call x1, Pallas kernels, local(): pl.pallas_call(functools.partial(kernel, dims), out_shape=(jax.ShapeDtype...  37 us
    pallas_call x1, Pallas kernels, local(): pl.pallas_call(update, out_shape=(like(alpha.shape, f32),) * 2 + (like(ow...  2.1 us

profile of v3, /device:TPU:0, one launch (start us, length us, event | category | flops | bytes accessed | tf_op | source)
XLA Modules:
  0.0 39.8 jit_solution(1885731672525765010)
XLA Ops:
  0.6 37.0 %analysis.1 = (f32[512,128]{1,0:T(8,128)}, f32[192,128]{1,0:T(8,128)}, f32[6,2,16,128]{3,2,1,0:T(8,128)}) custom-call(bf16[2,6,256,128]{3,2,1,0:T(8,128)(2,1)} %bitcast.7, f32[512,128]{1,0:T(8,128)} %bitcast.6, f32[32,128]{1,0:T(8,128)} %bitcast.10, f32[32,128]{1,0:T(8,128)} %bitcast.11, s32[1,1024]{1,0:T(1,128)} %cell_hbm.1, s32[1,1024]{1,0:T(1,128)} %mask_hbm.1, ...), custom_call_target="tpu_custom_call" | custom-call | tf_op jit(solution)/shard_map/analysis/pallas_call | solution.py:469
  37.7 2.1 %update.1 = (f32[2,16,16,128]{3,2,1,0:T(8,128)}, f32[2,16,16,128]{3,2,1,0:T(8,128)}, f32[6,2,16,128]{3,2,1,0:T(8,128)}, f32[6,2,16,128]{3,2,1,0:T(8,128)}) custom-call(f32[2,16,16,128]{3,2,1,0:T(8,128)} %field_a.1, f32[2,16,16,128]{3,2,1,0:T(8,128)} %mom_a.1, f32[2,16,16,128]{3,2,1,0:T(8,128)} %bitcast.8, f32[6,2,16,128]{3,2,1,0:T(8,128)} %get-tuple-element.8.field_s, ...), custom_call_target="tpu_custom_call" | custom-call | tf_op jit(solution)/shard_map/update/pallas_call | solution.py:535
